TPU v7x, 256 devices: a whole 4x4x8 slice. The times are simulated.
256 devices in a mesh: feat: 16 (over y_lo, x, core), batch: 16 (over y_hi, z).
Axes of the slice: x: 4, y: 4 (y_hi: 2, y_lo: 2; y = y_hi * 2 + y_lo), z: 8, core: 2. Of those that a mesh axis runs over, the one named last changes fastest.
Arguments:
- features: bfloat16 [131072, 4096], P('batch', 'feat'), may hold values from -6 to 6
- src_tile: int32 [256, 2], P('batch'), may hold values from 0 to 7
- rel_type: int32 [256, 2], P('batch'), may hold values from 0 to 3
- timestamps: int32 [32768], P(('batch', 'feat')), may hold values from 0 to 127
- edge_tiles: bfloat16 [4, 128, 1024], replicated, may hold values from -0.1875 to 0.1875
- rel_weight: bfloat16 [4, 4096, 512], P(None, 'feat'), may hold values from -0.09375 to 0.09375
- attn_gain: float32 [512], replicated, may hold values from 0.1 to 1.9
- w_qkv: bfloat16 [512, 1536], replicated, as said below
- w_out: bfloat16 [512, 512], replicated, may hold values from -0.25 to 0.25
- cotangent: bfloat16 [32768, 512], P(('batch', 'feat')), may hold values from -96 to 96
Outputs:
- layer_out: bfloat16 [32768, 512], P(('batch', 'feat'))
- grad_qkv: bfloat16 [512, 1536], replicated
- grad_out: bfloat16 [512, 512], replicated
- grad_gain: bfloat16 [512], replicated
- grad_rel: bfloat16 [4, 4096, 512], P(None, 'feat')
Inputs may be any that keep to these rules, and one draw needn't show every extreme that they name: `src_tile`: index of a source tile within the batch group. `w_qkv`: query, key and value columns in that order along the second dimension.
All inputs are finite; a program needn't handle non-finite values.
Results may differ from a plain program's by a relative error of at most 0.014.
Values may be sent and summed in bfloat16 or wider, within the bound.
No kernel may reach another device: no remote copies, remote signals or barrier semaphores. Data moves between devices by JAX's collectives and lax.ppermute only.
A program may use at most 128 MiB of HBM per device.

v0:
```python
import math
import jax
import jax.numpy as jnp
from jax import lax
from jax.sharding import PartitionSpec as P

D = 512
HEADS = 8
HEAD_DIM = 64
NREL = 4
SLOTS = 2
SBLK = 1024
EPS = 1e-06


def in_blocks(x, dim, devices):
    before, after = (x.shape[:dim], x.shape[dim + 1 :])
    return jnp.moveaxis(x.reshape(*before, devices, -1, *after), dim, 0)


def summed_on_arrival(x, axis, dim):
    pieces = in_blocks(x, dim, lax.axis_size(axis))
    arrived = lax.all_to_all(pieces, axis, split_axis=0, concat_axis=0, tiled=True)
    return arrived.sum(axis=0)


def aggregate(feats, sources_all, kinds_all, edge_tiles):

    def one_block(pair):
        sources, kinds = pair
        parts = []
        for slot in range(SLOTS):
            piece = lax.dynamic_slice_in_dim(feats, sources[slot] * SBLK, SBLK, 0)
            tile = lax.dynamic_index_in_dim(edge_tiles, kinds[slot], 0, keepdims=False)
            parts.append(jnp.dot(tile, piece, preferred_element_type=jnp.float32))
        member = (kinds[:, None] == jnp.arange(NREL, dtype=jnp.int32)[None, :]).astype(jnp.float32)
        merged = member[0][:, None, None] * parts[0][None]
        slot = 1
        merged = merged + member[slot][:, None, None] * parts[slot][None]
        return merged.astype(jnp.bfloat16)

    blocks = lax.map(one_block, (sources_all, kinds_all))
    return jnp.moveaxis(blocks, 1, 0).reshape(NREL, -1, feats.shape[1])


def layer_forward(tokens, gain, w_qkv, w_out, times):
    token_values = tokens.astype(jnp.float32)
    scale = lax.rsqrt(jnp.mean(token_values * token_values, axis=-1, keepdims=True) + EPS)
    normed = (token_values * scale * gain).astype(jnp.bfloat16)
    projected = jnp.dot(normed, w_qkv, preferred_element_type=jnp.float32).astype(jnp.bfloat16)
    length = tokens.shape[0]
    queries = projected[:, :D].reshape(length, HEADS, HEAD_DIM)
    keys = projected[:, D : 2 * D].reshape(length, HEADS, HEAD_DIM)
    contents = projected[:, 2 * D :].reshape(length, HEADS, HEAD_DIM)
    scores = jnp.einsum(
        "qhd,khd->hqk", queries, keys, preferred_element_type=jnp.float32
    ) / math.sqrt(HEAD_DIM)
    allowed = times[None, :] <= times[:, None]
    scores = jnp.where(allowed[None], scores, -1e30)
    weights = jax.nn.softmax(scores, axis=-1).astype(jnp.bfloat16)
    context = jnp.einsum("hqk,khd->qhd", weights, contents, preferred_element_type=jnp.float32)
    context = context.astype(jnp.bfloat16).reshape(length, D)
    return (token_values + jnp.dot(context, w_out, preferred_element_type=jnp.float32)).astype(
        jnp.bfloat16
    )


def silu_slope(total):
    sigma = jax.nn.sigmoid(total)
    return sigma * (1.0 + total * (1.0 - sigma))


def project_one(relations, rel_weight, relation, start, count):
    rows_part = lax.dynamic_slice_in_dim(relations[relation], start, count, 0)
    return jnp.dot(rows_part, rel_weight[relation], preferred_element_type=jnp.float32)


def project_every(relations, rel_weight, start, count):
    summed = project_one(relations, rel_weight, 0, start, count)
    for relation in range(1, NREL):
        summed = summed + project_one(relations, rel_weight, relation, start, count)
    return summed


def shards(
    features,
    src_tile,
    rel_type,
    timestamps,
    edge_tiles,
    rel_weight,
    attn_gain,
    w_qkv,
    w_out,
    cotangent,
):
    relations = aggregate(features, src_tile, rel_type, edge_tiles)
    own_rows = timestamps.shape[0]
    total = summed_on_arrival(
        project_every(relations, rel_weight, jnp.int32(0), own_rows * lax.axis_size("feat")),
        "feat",
        0,
    )
    hidden = jax.nn.silu(total).astype(jnp.bfloat16)
    layer_out, pullback = jax.vjp(
        lambda a, b, c, d: layer_forward(a, b, c, d, timestamps), hidden, attn_gain, w_qkv, w_out
    )
    d_hidden, d_gain, d_qkv, d_out = pullback(cotangent)
    d_total = (d_hidden.astype(jnp.float32) * silu_slope(total)).astype(jnp.bfloat16)
    piece = lax.all_gather(d_total, "feat", axis=0, tiled=True)
    columns = lax.slice_in_dim(relations, 0, piece.shape[0], axis=1)
    rel_terms = lax.dot_general(
        columns, piece, (((1,), (0,)), ((), ())), preferred_element_type=jnp.float32
    )
    grad_rel = lax.psum(rel_terms, "batch").astype(jnp.bfloat16)
    terms = (d_qkv.astype(jnp.float32), d_out.astype(jnp.float32), d_gain)
    sums = lax.psum((terms[0], terms[1], terms[2]), ("feat", "batch"))
    grad_qkv = sums[0].astype(jnp.bfloat16)
    grad_out = sums[1].astype(jnp.bfloat16)
    grad_gain = sums[2].astype(jnp.bfloat16)
    return (layer_out, grad_qkv, grad_out, grad_gain, grad_rel)


def solution(mesh):
    in_specs = (
        P("batch", "feat"),
        P("batch", None),
        P("batch", None),
        P(("batch", "feat")),
        P(),
        P(None, "feat", None),
        P(),
        P(),
        P(),
        P(("batch", "feat"), None),
    )
    out_specs = (P(("batch", "feat"), None), P(), P(), P(), P(None, "feat", None))
    return jax.shard_map(shards, mesh=mesh, in_specs=in_specs, out_specs=out_specs, check_vma=False)
```

profile of v0, /device:TPU:16, one launch (start us, length us, event | category | flops | bytes accessed | tf_op | source)
XLA Modules:
  0.0 512.9 jit_solution(11323617679978035870)
XLA Ops:
  8.1 171.9 %while.10 = (s32[]{:T(128)}, bf16[16,4,128,256]{3,2,0,1:T(8,128)(2,1)}, s32[16,2]{1,0:T(8,128)S(1)}, bf16[4,128,1024]{2,1,0:T(8,128)(2,1)}, s32[16,2]{0,1:T(2,12...) while((s32[]{:T(128)}, ...), condition=%wide.region_1.2_spmd, body=%wide.region_0.1_spmd.sunk | while | flops 134742048 | bytes 2360321 | solution.py:42
  12.5 1.4 fusion.102
  23.3 1.4 fusion.102
  34.0 1.4 fusion.102
  44.8 1.4 fusion.102
  55.5 1.4 fusion.102
  66.3 1.4 fusion.102
  77.0 1.4 fusion.102
  130.7 1.4 fusion.102
  152.2 1.4 fusion.102
  179.9 2.7 fusion.51
  184.8 2.7 add_add_fusion
  187.6 5.3 %all-to-all-start = ((f32[16,128,512]{2,1,0:T(8,128)}), f32[16,128,512]{2,1,0:T(8,128)}, u32[]{:S(2)}, u32[]{:S(2)}) async-start(f32[16,128,512]{2,1,0:T(8,128)} %bitcast.108), calls=%async_computation | async-start | bytes 8388608 | tf_op jit(solution)/shard_map/all_to_all | solution.py:23
  194.1 55.0 %all-to-all-done = f32[16,128,512]{2,1,0:T(8,128)} async-done(((f32[16,128,512]{2,1,0:T(8,128)}), f32[16,128,512]{2,1,0:T(8,128)}, u32[]{:S(2)}, u32[]{:S(2)}) %all-to-all-start) | async-done | bytes 4194336 | tf_op jit(solution)/shard_map/all_to_all | solution.py:23
  249.1 2.6 reduce_sum.51
  253.2 1.9 fusion.53
  256.5 2.1 multiply_reduce_fusion
  258.6 1.6 convolution_convert_fusion.5
  260.3 1.6 convolution_convert_fusion.4
  263.6 2.3 fusion.13
  265.9 1.5 convolution_convert_fusion.8
  268.6 138.7 %all-reduce.7 = (bf16[512,1536]{1,0:T(8,128)(2,1)}, bf16[512,512]{1,0:T(8,128)(2,1)}, bf16[512]{0:T(512)(128)(2,1)}) all-reduce(f32[512,1536]{1,0:T(8,128)} %fusion.13, f32[512,512]{1,0:T(8,128)S(1)} %fusion.17, f32[512]{0:T(512)S(1)} %get-tuple-element.51), channel_id=1, replica_groups=mesh['feat'=16,'batch'=16] {'feat','batch'}, use_global_device_ids=true, to_apply=%region_7.8 | all-reduce | flops 1049088 | bytes 6294528 | tf_op jit(solution)/shard_map/psum | solution.py:117
  407.3 6.6 %fusion.14 = f32[4,256,512]{2,1,0:T(8,128)} fusion(bf16[4,2048,256]{2,1,0:T(8,128)(2,1)} %bitcast.110, bf16[2048,512]{1,0:T(8,128)(2,1)} %all-gather.2.cloned.1.call-done), kind=kOutput, calls=%fused_computation.23 | convolution fusion | flops 2147483648 | bytes 8388608 | tf_op jit(solution)/shard_map/dot_general | solution.py:112
  413.9 92.2 %all-reduce.6 = bf16[4,256,512]{2,1,0:T(8,128)(2,1)} all-reduce(f32[4,256,512]{2,1,0:T(8,128)} %fusion.14), channel_id=1, replica_groups=mesh['feat'=16,'batch'=16] {'batch'}, use_global_device_ids=true, to_apply=%region_12.13 | all-reduce | flops 524288 | bytes 3145728 | tf_op jit(solution)/shard_map/psum | solution.py:115
  (197 shorter events, 85.8 us)
Async XLA Ops:
  7.2 245.3 %copy-start = (bf16[512,1536]{1,0:T(8,128)(2,1)S(1)}, bf16[512,1536]{1,0:T(8,128)(2,1)}, u32[]{:S(2)}) copy-start(bf16[512,1536]{1,0:T(8,128)(2,1)} %param.19) | copy-start | bytes 4718596
  179.9 2.8 copy-start.3
  187.6 5.4 %copy-start.1 = (bf16[512,512]{1,0:T(8,128)(2,1)S(1)}, bf16[512,512]{1,0:T(8,128)(2,1)}, u32[]{:S(2)}) copy-start(bf16[512,512]{1,0:T(8,128)(2,1)} %param.20) | copy-start | bytes 1572868
  187.6 5.4 %copy-start.2 = (bf16[128,512]{1,0:T(8,128)(2,1)S(1)}, bf16[128,512]{1,0:T(8,128)(2,1)}, u32[]{:S(2)}) copy-start(bf16[128,512]{1,0:T(8,128)(2,1)} %param.21) | copy-start | bytes 393220
  187.6 5.8 %copy-start.7 = (s32[128]{0:T(128)S(1)}, s32[128]{0:T(128)}, u32[]{:S(2)}) copy-start(s32[128]{0:T(128)} %param.15) | copy-start | bytes 1540
  187.6 61.6 %all-to-all-start = ((f32[16,128,512]{2,1,0:T(8,128)}), f32[16,128,512]{2,1,0:T(8,128)}, u32[]{:S(2)}, u32[]{:S(2)}) async-start(f32[16,128,512]{2,1,0:T(8,128)} %bitcast.108), calls=%async_computation | async-start | bytes 8388608 | tf_op jit(solution)/shard_map/all_to_all | solution.py:23
  192.9 59.6 %copy-start.6 = (f32[512]{0:T(512)S(1)}, f32[512]{0:T(512)}, u32[]{:S(2)}) copy-start(f32[512]{0:T(512)} %param.18) | copy-start | bytes 6148
  192.9 214.4 %all-gather.2.cloned.1.call-start = ((), (), s32[]{:S(2)}) async-start(), calls=%async_computation.1 | async-start | bytes 2228224 | tf_op jit(solution)/shard_map/all_gather | solution.py:110
  251.9 0.5 copy-start.8
  253.0 7.2 %copy-start.4 = (bf16[128,512]{0,1:T(8,128)(2,1)}, bf16[128,512]{0,1:T(8,128)(2,1)S(1)}, u32[]{:S(2)}) copy-start(bf16[128,512]{0,1:T(8,128)(2,1)S(1)} %copy.30) | copy-start | bytes 393220
  253.2 7.1 %copy-start.5 = (bf16[128,512]{0,1:T(8,128)(2,1)}, bf16[128,512]{0,1:T(8,128)(2,1)S(1)}, u32[]{:S(2)}) copy-start(bf16[128,512]{0,1:T(8,128)(2,1)S(1)} %copy.31) | copy-start | bytes 393220
  258.6 4.0 copy-start.9
Sparse Core Ops, SparseCore 0:
  263.7 39.7 all-gather.1
where the time goes:
time: 516 us; the launch traced here: 513 us
  blocking collectives  231 us (45%)
  loops' own time  83.6 us (16%)
  matrix products  70 us (14%)
  waiting for transfers between devices  55.1 us (11%)
  local copies, waits for them, and re-layouts  34.8 us (7%)
  other arithmetic  18.9 us (4%)
  between operations  14.3 us (3%)
  starting transfers between devices  5.35 us (1%)
    psum x1, blocking collectives, shards(): sums = lax.psum((terms[0], terms[1], terms[2]), ('feat', 'batch'))  139 us
    psum x1, blocking collectives, shards(): grad_rel = lax.psum(rel_terms, 'batch').astype(jnp.bfloat16)  92.2 us
    another operation x1, loops' own time, aggregate(): blocks = lax.map(one_block, (sources_all, kinds_all))  83.6 us
    all_to_all x1, waiting for transfers between devices, summed_on_arrival(): lax.all_to_all(pieces, axis, split_axis=0, concat_axis=0, tiled=True)  55 us
    dot_general x32, matrix products, one_block(): parts.append(jnp.dot(tile, piece, preferred_element_type=jnp.float32))  43.6 us
    dynamic_update_slice x16, other arithmetic, aggregate(): blocks = lax.map(one_block, (sources_all, kinds_all))  13.4 us
    dynamic_slice x32, local copies, waits for them, and re-layouts, aggregate(): blocks = lax.map(one_block, (sources_all, kinds_all))  12.2 us
  transfers between devices with their start and end apart: 2, of which 1 were waited for; matrix products, arithmetic and copies ran while one was open for 1% of the time, Pallas kernels for 0%

commit v1 on v0

--- a/solution.py
+++ b/solution.py
@@ -11,6 +11,11 @@
 SLOTS = 2
 SBLK = 1024
 EPS = 1e-06
+
+
+def gather_and_add(array, name):
+    parts = lax.all_gather(array, name)
+    return jnp.sum(parts, axis=0)
 
 
 def in_blocks(x, dim, devices):
@@ -112,7 +117,7 @@
     rel_terms = lax.dot_general(
         columns, piece, (((1,), (0,)), ((), ())), preferred_element_type=jnp.float32
     )
-    grad_rel = lax.psum(rel_terms, "batch").astype(jnp.bfloat16)
+    grad_rel = gather_and_add(rel_terms, "batch").astype(jnp.bfloat16)
     terms = (d_qkv.astype(jnp.float32), d_out.astype(jnp.float32), d_gain)
     sums = lax.psum((terms[0], terms[1], terms[2]), ("feat", "batch"))
     grad_qkv = sums[0].astype(jnp.bfloat16)

time: 516 us -> 763 us (1.48)
  waiting for transfers between devices: 55.1 us -> 182 us
  blocking collectives: 231 us -> 331 us
  other arithmetic: 18.9 us -> 32.8 us
    psum x1, blocking collectives: 139 us -> 331 us  [shards(): sums = lax.psum((terms[0], terms[1], terms[2]), ('feat', 'batch'))]
    psum x1 -> x0, blocking collectives: 92.2 us -> none  [shards(): grad_rel = lax.psum(rel_terms, 'batch').astype(jnp.bfloat16)]
    all_gather x0 -> x1, waiting for transfers between devices: none -> 89 us  [gather_and_add(): parts = lax.all_gather(array, name)]
    all_gather x1, waiting for transfers between devices: 0.01 us -> 38.3 us  [shards(): piece = lax.all_gather(d_total, 'feat', axis=0, tiled=True)]
    reduce_sum x0 -> x1, other arithmetic: none -> 13.8 us  [gather_and_add(): return jnp.sum(parts, axis=0)]
  transfers between devices with their start and end apart: 2 -> 3, of which waited for: 1 -> 3; matrix products, arithmetic and copies ran while one was open for 1% -> 1% of each run, Pallas kernels for 0% -> 0%
where the time goes in v1:
time: 763 us; the launch traced here: 755 us
  blocking collectives  331 us (43%)
  waiting for transfers between devices  182 us (24%)
  loops' own time  83.4 us (11%)
  matrix products  70.8 us (9%)
  local copies, waits for them, and re-layouts  34.7 us (5%)
  other arithmetic  32.8 us (4%)
  between operations  14.3 us (2%)
    psum x1, blocking collectives, shards(): sums = lax.psum((terms[0], terms[1], terms[2]), ('feat', 'batch'))  331 us
    all_gather x1, waiting for transfers between devices, gather_and_add(): parts = lax.all_gather(array, name)  89 us
    another operation x1, loops' own time, aggregate(): blocks = lax.map(one_block, (sources_all, kinds_all))  83.4 us
    all_to_all x1, waiting for transfers between devices, summed_on_arrival(): lax.all_to_all(pieces, axis, split_axis=0, concat_axis=0, tiled=True)  55.1 us
    dot_general x32, matrix products, one_block(): parts.append(jnp.dot(tile, piece, preferred_element_type=jnp.float32))  43.6 us
    all_gather x1, waiting for transfers between devices, shards(): piece = lax.all_gather(d_total, 'feat', axis=0, tiled=True)  38.3 us
  transfers between devices with their start and end apart: 3, of which 3 were waited for; matrix products, arithmetic and copies ran while one was open for 1% of the time, Pallas kernels for 0%

profile of v1, /device:TPU:16, one launch (start us, length us, event | category | flops | bytes accessed | tf_op | source)
XLA Modules:
  0.0 754.6 jit_solution(4720020433054538425)
XLA Ops:
  8.1 171.6 %while.10 = (s32[]{:T(128)}, bf16[16,4,128,256]{3,2,0,1:T(8,128)(2,1)}, s32[16,2]{1,0:T(8,128)S(1)}, bf16[4,128,1024]{2,1,0:T(8,128)(2,1)}, s32[16,2]{0,1:T(2,12...) while((s32[]{:T(128)}, ...), condition=%wide.region_1.2_spmd, body=%wide.region_0.1_spmd.sunk | while | flops 134742048 | bytes 2359821 | solution.py:47
  16.6 1.4 fusion.102
  27.3 1.4 fusion.102
  38.0 1.4 fusion.102
  48.7 1.4 fusion.102
  59.5 1.4 fusion.102
  113.1 1.4 fusion.102
  123.8 1.4 fusion.102
  177.4 1.4 fusion.102
  179.7 2.7 fusion.51
  184.5 2.7 add_add_fusion
  187.3 5.3 all-to-all-start
  193.8 55.1 %all-to-all-done = f32[16,128,512]{2,1,0:T(8,128)} async-done(((f32[16,128,512]{2,1,0:T(8,128)}), f32[16,128,512]{2,1,0:T(8,128)}, u32[]{:S(2)}, u32[]{:S(2)}) %all-to-all-start) | async-done | bytes 4194336 | tf_op jit(solution)/shard_map/all_to_all | solution.py:28
  248.9 2.6 reduce_sum.62
  253.0 1.9 fusion.53
  256.2 2.2 multiply_reduce_fusion
  258.4 1.6 convolution_convert_fusion.4
  260.0 1.7 convolution_convert_fusion.5
  263.4 38.3 %all-gather.4.cloned.1.call-done = bf16[2048,512]{1,0:T(8,128)(2,1)} async-done(((bf16[128,512]{1,0:T(8,128)(2,1)}), bf16[2048,512]{1,0:T(8,128)(2,1)}) %all-gather.4.cloned.1.call-update) | async-done | bytes 2097168 | tf_op jit(solution)/shard_map/all_gather | solution.py:115
  301.8 6.6 fusion.14
  310.0 3.3 fusion.13
  314.2 330.8 %all-reduce.5 = (bf16[512,1536]{1,0:T(8,128)(2,1)}, bf16[512,512]{1,0:T(8,128)(2,1)}, bf16[512]{0:T(512)(128)(2,1)}) all-reduce(f32[512,1536]{1,0:T(8,128)} %fusion.13, f32[512,512]{1,0:T(8,128)S(1)} %fusion.17, f32[512]{0:T(512)S(1)} %get-tuple-element.57), channel_id=1, replica_groups=mesh['feat'=16,'batch'=16] {'feat','batch'}, use_global_device_ids=true, to_apply=%region_7.8 | all-reduce | flops 1049088 | bytes 6294528 | tf_op jit(solution)/shard_map/psum | solution.py:122
  645.0 89.0 %all-gather.6.cloned.1.call-done = f32[64,256,512]{2,1,0:T(8,128)} async-done(((f32[4,256,512]{2,1,0:T(8,128)}), f32[64,256,512]{2,1,0:T(8,128)}) %all-gather.6.cloned.1.call-update) | async-done | bytes 33554448 | tf_op jit(solution)/shard_map/all_gather | solution.py:17
  733.9 13.8 %reduce_sum.81 = bf16[4,256,512]{2,1,0:T(8,128)(2,1)} reduce(f32[16,4,256,512]{3,2,1,0:T(8,128)} %bitcast.109, f32[]{:T(128)} %constant.33.clone.1), dimensions={0}, to_apply=%region_12.13 | reduce | flops 7864320 | bytes 34603012 | tf_op jit(solution)/shard_map/reduce_sum | solution.py:18
  (210 shorter events, 88.3 us)
Async XLA Ops:
  7.2 245.0 %copy-start = (bf16[512,1536]{1,0:T(8,128)(2,1)S(1)}, bf16[512,1536]{1,0:T(8,128)(2,1)}, u32[]{:S(2)}) copy-start(bf16[512,1536]{1,0:T(8,128)(2,1)} %param.19) | copy-start | bytes 4718596
  179.7 2.8 copy-start.3
  187.3 5.4 copy-start.1
  187.3 5.4 copy-start.2
  187.3 5.8 copy-start.12
  187.3 61.6 %all-to-all-start = ((f32[16,128,512]{2,1,0:T(8,128)}), f32[16,128,512]{2,1,0:T(8,128)}, u32[]{:S(2)}, u32[]{:S(2)}) async-start(f32[16,128,512]{2,1,0:T(8,128)} %bitcast.110), calls=%async_computation | async-start | bytes 8388608 | tf_op jit(solution)/shard_map/all_to_all | solution.py:28
  192.6 59.6 %copy-start.11 = (f32[512]{0:T(512)S(1)}, f32[512]{0:T(512)}, u32[]{:S(2)}) copy-start(f32[512]{0:T(512)} %param.18) | copy-start | bytes 6148
  192.6 109.2 %all-gather.4.cloned.1.call-start = ((), (), s32[]{:S(2)}) async-start(), calls=%async_computation.1 | async-start | bytes 2228224 | tf_op jit(solution)/shard_map/all_gather | solution.py:115
  251.7 0.5 copy-start.13
  252.8 7.2 copy-start.7
  252.9 7.1 copy-start.9
  256.2 6.3 copy-start.4
  258.4 4.1 copy-start.14
  260.0 48.4 %copy-start.5 = (bf16[8,128,64]{1,2,0:T(8,128)(2,1)}, bf16[8,128,64]{1,2,0:T(8,128)(2,1)S(1)}, u32[]{:S(2)}) copy-start(bf16[8,128,64]{1,2,0:T(8,128)(2,1)S(1)} %convolution_convert_fusion.4) | copy-start | bytes 393220
  261.7 46.7 %copy-start.6 = (bf16[8,128,64]{1,2,0:T(8,128)(2,1)}, bf16[8,128,64]{1,2,0:T(8,128)(2,1)S(1)}, u32[]{:S(2)}) copy-start(bf16[8,128,64]{1,2,0:T(8,128)(2,1)S(1)} %convolution_convert_fusion.5) | copy-start | bytes 393220
  263.4 470.5 %all-gather.6.cloned.1.call-start = ((), (), s32[]{:S(2)}) async-start(), calls=%async_computation.2 | async-start | bytes 35651584 | tf_op jit(solution)/shard_map/all_gather | solution.py:17
  301.8 6.7 copy-start.8
  301.8 6.7 copy-start.10
Sparse Core Ops, SparseCore 0:
  263.5 38.2 all-gather.3
  308.6 425.3 all-gather.5
